TPU v7x, 32 devices: a whole 2x2x4 slice. The times are simulated.
32 devices in a mesh: grp: 2 (over y), ep: 4 (over z), tp: 4 (over x, core).
Axes of the slice: x: 2, y: 2, z: 4, core: 2. Of those that a mesh axis runs over, the one named last changes fastest.
Arguments:
- question_q: bfloat16 [1024, 32, 128], P(('grp', 'ep'), 'tp'), parts along dimension 0, may hold values from -125 to 125
- question_kv: bfloat16 [1024, 4, 2, 128], P(('grp', 'ep')), parts along dimension 0, may hold values from -6 to 6
- doc_kv: bfloat16 [16, 128, 4, 2, 128], P(('grp', 'ep')), parts along dimension 0, may hold values from -6 to 6
- doc_lens: int32 [16], P('grp'), parts along dimension 0, may hold values from 1 to 128, as said below
- query_docs: int32 [8, 4], P('grp'), parts along dimension 0, may hold values from 0 to 7, as said below
- ctx_pos: int32 [8, 5], P('grp'), parts along dimension 0, may hold values from 0 to 827, as said below
- hidden: bfloat16 [1024, 4096], P(('grp', 'ep'), 'tp'), parts along dimension 0, may hold values from -1.5 to 1.5
- out_proj: bfloat16 [4096, 4096], P('ep', 'tp'), may hold values from -0.0234375 to 0.0234375
- norm_gain: bfloat16 [4096], P('tp'), may hold values from 0.5 to 1.5
- router_weight: bfloat16 [4096, 16], P('tp'), may hold values from -0.046875 to 0.046875
- w_gate_up: bfloat16 [16, 4096, 2, 1024], P('ep', 'tp'), may hold values from -0.09375 to 0.09375
- w_down: bfloat16 [16, 1024, 4096], P('ep', None, 'tp'), may hold values from -0.1875 to 0.1875
- expert_ids: int32 [1024, 8], P(('grp', 'ep')), parts along dimension 0, may hold values from 0 to 15, all different within a row; in each aligned block of 128 rows (0 to 127, 128 to 255, ...) at most 64 rows name the same one
Outputs:
- layer_out: bfloat16 [1024, 4096], P(('grp', 'ep'), 'tp'), parts along dimension 0
There are 2 independent parts, one for each index of `grp`. A program takes and returns all parts, laid end to end along the dimension named above; an argument that names none is the same for every part. Nothing has to cross between parts.
Inputs may be any that keep to these rules, and one draw needn't show every extreme that they name: `doc_lens`: document d is held at row d of doc_kv; some document of some query's list has exactly 128 tokens. `query_docs`: the 4 documents of a query lie in 4 different blocks of 2 consecutive documents. `ctx_pos`: in each row, every entry is at least the one before it plus the length of the document before it. `expert_ids`: each query's 128 tokens name every expert exactly 64 times.
All inputs are finite; a program needn't handle non-finite values.
Results may differ from a plain program's by a relative error of at most 0.017.
Values may be sent and summed in bfloat16 or wider, within the bound.
A program may use at most 128 MiB of HBM per device.

v0:
```python
import math

import jax
import jax.numpy as jnp
from jax import lax
from jax.sharding import PartitionSpec as P

D = 4096
HID = 1024


rope_theta = 1000000.0
norm_eps = 1e-06


def narrow(values):
    return lax.optimization_barrier(values.astype(jnp.bfloat16))


def rotate(values, positions):
    half = values.shape[-1] // 2
    freq = jnp.exp(
        jnp.arange(half, dtype=jnp.float32) * (-2.0 * math.log(rope_theta) / values.shape[-1])
    )
    angle = positions.astype(jnp.float32)[:, None] * freq[None, :]
    shape = (values.shape[0],) + (1,) * (values.ndim - 2) + (half,)
    cosine = jnp.cos(angle).reshape(shape)
    sine = jnp.sin(angle).reshape(shape)
    floats = values.astype(jnp.float32)
    first = floats[..., :half]
    second = floats[..., half:]
    return jnp.concatenate(
        [first * cosine - second * sine, second * cosine + first * sine], axis=-1
    )


def fetch_context(doc_kv, doc_lens, query_docs, row_pos, device, kv_pick):
    pool_dev, doc_max, kv_heads, pair, head_dim = doc_kv.shape
    docs_per = query_docs.shape[1]
    pool_head = lax.dynamic_index_in_dim(doc_kv, kv_pick, 2, keepdims=False).reshape(
        pool_dev, doc_max, pair * head_dim
    )
    held = device * pool_dev + jnp.arange(pool_dev, dtype=jnp.int32)
    wanted = jnp.sum((query_docs[:, :, None] == held[None, None, :]).astype(jnp.float32), axis=1)
    sending = jnp.einsum(
        "rl,lkc->rkc", wanted.astype(jnp.bfloat16), pool_head, preferred_element_type=jnp.float32
    ).astype(jnp.bfloat16)
    received = lax.all_to_all(sending, "ep", split_axis=0, concat_axis=0, tiled=True)
    my_docs = lax.dynamic_index_in_dim(query_docs, device, 0, keepdims=False)
    context = jnp.take(received, my_docs // pool_dev, axis=0)
    lengths = jnp.take(doc_lens, my_docs)
    positions = jnp.repeat(row_pos[:docs_per], doc_max, total_repeat_length=docs_per * doc_max)
    keys = rotate(context[:, :, :head_dim].reshape(docs_per * doc_max, head_dim), positions).astype(
        jnp.bfloat16
    )
    values = context[:, :, head_dim:].reshape(docs_per * doc_max, head_dim)
    valid = (jnp.arange(doc_max, dtype=jnp.int32)[None, :] < lengths[:, None]).reshape(
        docs_per * doc_max
    )
    return (keys, values, valid)


def per_device(
    question_q,
    question_kv,
    doc_kv,
    doc_lens,
    query_docs,
    ctx_pos,
    hidden,
    out_proj,
    norm_gain,
    router_weight,
    w_gate_up,
    w_down,
    expert_ids,
):
    lanes = lax.axis_size("tp")
    groups = lax.axis_size("ep")
    lane = lax.axis_index("tp")
    device = lax.axis_index("ep")
    length, heads_here, head_dim = question_q.shape
    kv_heads = question_kv.shape[1]
    kv_pick = lane * kv_heads // lanes
    scale = head_dim ** (-0.5)
    docs_per = query_docs.shape[1]
    row_pos = lax.dynamic_index_in_dim(ctx_pos, device, 0, keepdims=False)
    question_pos = row_pos[docs_per] + jnp.arange(length, dtype=jnp.int32)
    queries = rotate(question_q, question_pos).astype(jnp.bfloat16)
    own_kv = lax.dynamic_index_in_dim(question_kv, kv_pick, 1, keepdims=False)
    own_keys = rotate(own_kv[:, 0], question_pos).astype(jnp.bfloat16)
    own_values = own_kv[:, 1]
    causal = jnp.arange(length)[:, None] >= jnp.arange(length)[None, :]
    doc_keys, doc_values, valid = fetch_context(
        doc_kv, doc_lens, query_docs, row_pos, device, kv_pick
    )
    keys = jnp.concatenate([doc_keys, own_keys], axis=0)
    values = jnp.concatenate([doc_values, own_values], axis=0)
    allowed = jnp.concatenate(
        [jnp.broadcast_to(valid[None, :], (length, valid.shape[0])), causal], axis=1
    )
    scores = jnp.einsum("ihd,jd->hij", queries, keys, preferred_element_type=jnp.float32) * scale
    scores = jnp.where(allowed[None], scores, -jnp.inf)
    ceiling = jnp.max(scores, axis=-1, keepdims=True)
    probs = jnp.exp(scores - ceiling)
    denominator = jnp.sum(probs, axis=-1, keepdims=True)
    mixed = jnp.einsum(
        "hij,jd->hid", probs.astype(jnp.bfloat16), values, preferred_element_type=jnp.float32
    )
    attended = (
        jnp.transpose(mixed / denominator, (1, 0, 2))
        .reshape(length, heads_here * head_dim)
        .astype(jnp.bfloat16)
    )
    all_heads = lax.all_gather(attended, "tp", axis=1, tiled=True)
    width_here = hidden.shape[1]
    projected = jnp.dot(
        all_heads,
        lax.all_gather(out_proj, "ep", axis=0, tiled=True),
        preferred_element_type=jnp.float32,
    )
    residual_wide = narrow(hidden.astype(jnp.float32) + projected).astype(jnp.float32)
    gain = norm_gain.astype(jnp.float32)
    squares, logit_part = lax.psum(
        (
            jnp.sum(residual_wide * residual_wide, axis=1),
            jnp.dot(
                residual_wide * gain[None, :],
                router_weight.astype(jnp.float32),
                precision=lax.Precision.HIGHEST,
            ),
        ),
        "tp",
    )
    inv_rms = lax.rsqrt(squares / D + norm_eps)
    normed = (residual_wide * inv_rms[:, None] * gain[None, :]).astype(jnp.bfloat16)
    logits = logit_part * inv_rms[:, None]
    mix = jax.nn.softmax(jnp.take_along_axis(logits, expert_ids, axis=1), axis=1)
    local_experts = w_gate_up.shape[0]
    experts = local_experts * groups
    choose = expert_ids.shape[1]
    slots = length * choose
    capacity = slots // experts
    flat_ids = expert_ids.reshape(slots)
    onehot = (flat_ids[:, None] == jnp.arange(experts, dtype=jnp.int32)[None, :]).astype(jnp.int32)
    rank = jnp.sum(jnp.cumsum(onehot, axis=0) * onehot, axis=1) - 1
    position = flat_ids * capacity + rank
    source_row = (
        jnp.zeros((slots,), jnp.int32)
        .at[position]
        .set(jnp.arange(slots, dtype=jnp.int32) // choose)
    )
    sending = jnp.take(normed, source_row, axis=0)
    arrived = lax.all_to_all(sending, "ep", split_axis=0, concat_axis=0, tiled=True).reshape(
        groups, local_experts, capacity, width_here
    )
    hidden_here = HID // lanes
    piece = w_gate_up
    term = jnp.einsum("secd,edgh->hegsc", arrived, piece, preferred_element_type=jnp.float32)
    summed = lax.psum_scatter(
        term.reshape(lax.axis_size("tp") * hidden_here, local_experts, 2, groups * capacity).astype(
            jnp.bfloat16
        ),
        "tp",
        scatter_dimension=0,
        tiled=True,
    ).astype(jnp.float32)
    activated = (jax.nn.silu(summed[:, :, 0]) * summed[:, :, 1]).astype(jnp.bfloat16)
    piece = lax.all_gather(activated, "tp", axis=0, tiled=True)
    count = piece.shape[0]
    expert_out = jnp.einsum(
        "hesc,ehd->secd",
        piece.reshape(count, local_experts, groups, capacity),
        w_down,
        preferred_element_type=jnp.float32,
    )
    returned = lax.all_to_all(
        expert_out.astype(jnp.bfloat16), "ep", split_axis=0, concat_axis=0, tiled=True
    ).reshape(slots, width_here)
    gathered = jnp.take(returned, position, axis=0).reshape(length, choose, width_here)
    combined = jnp.einsum("tk,tkd->td", mix, gathered.astype(jnp.float32))
    return (residual_wide + combined).astype(jnp.bfloat16)


def solution(mesh):
    placed = (
        P(("grp", "ep"), "tp", None),
        P(("grp", "ep"), None, None, None),
        P(("grp", "ep"), None, None, None, None),
        P("grp"),
        P("grp", None),
        P("grp", None),
        P(("grp", "ep"), "tp"),
        P("ep", "tp"),
        P("tp"),
        P("tp", None),
        P("ep", "tp", None, None),
        P("ep", None, "tp"),
        P(("grp", "ep"), None),
    )
    return jax.shard_map(
        per_device, mesh=mesh, in_specs=placed, out_specs=P(("grp", "ep"), "tp"), check_vma=False
    )
```

profile of v0, /device:TPU:0, one launch (start us, length us, event | category | flops | bytes accessed | tf_op | source)
XLA Modules:
  0.0 429.1 jit_solution(6567068346125474226)
XLA Ops:
  6.5 1.0 copy-done
  7.8 0.8 convert_reduce_fusion
  9.0 0.7 copy.90
  9.7 6.3 %all-to-all-start = ((bf16[4,128,256]{2,1,0:T(8,128)(2,1)}), bf16[4,128,256]{2,1,0:T(8,128)(2,1)S(1)}, u32[]{:S(2)}, u32[]{:S(2)}) async-start(bf16[4,128,256]{2,1,0:T(8,128)(2,1)} %copy.90), calls=%async_computation | async-start | bytes 524288 | tf_op jit(solution)/shard_map/all_to_all | solution.py:48
  16.1 0.7 fusion.71
  18.2 2.5 compare_select_fusion.5
  20.7 0.9 constant_dynamic-slice_fusion
  24.1 0.9 all-to-all-done
  28.0 1.5 fusion.24
  29.6 0.7 all-gather.6.cloned.1.call-update
  30.7 4.5 %reduce-window.14 = s32[16,8,128]{2,1,0:T(8,128)S(1)} reduce-window(s32[16,8,128]{2,1,0:T(8,128)S(1)} %fusion.59, s32[]{:T(128)} %constant.209.clone.1), window={size=1x1x128 pad=0_0x0_0x127_0}, to_apply=%region_8.9 | reduce-window | flops 2080768 | bytes 131076 | tf_op jit(solution)/shard_map/reduce-window.3
  35.9 4.3 %scatter_custom_fusion = s32[1024]{0:T(1024)S(1)} fusion(s32[1024]{0:T(1024)S(1)} %bitcast.163, s32[1024]{0:T(1024)S(1)} %add_select_fusion, s32[]{:T(128)} %constant.209.clone.1), kind=kCustom, calls=%fused_computation.122 | custom fusion | bytes 4100 | tf_op jit(solution)/shard_map/scatter | solution.py:151
  40.3 6.7 %all-gather.4.cloned.1.call-done = bf16[128,4096]{0,1:T(8,128)(2,1)} async-done(((bf16[128,1024]{0,1:T(8,128)(2,1)}), bf16[128,4096]{0,1:T(8,128)(2,1)}) %all-gather.4.cloned.1.call-update) | async-done | bytes 1048592 | tf_op jit(solution)/shard_map/all_gather | solution.py:115
  47.0 151.2 %all-gather.6.cloned.1.call-done = bf16[4096,1024]{1,0:T(8,128)(2,1)} async-done(((bf16[1024,1024]{1,0:T(8,128)(2,1)}), bf16[4096,1024]{1,0:T(8,128)(2,1)}) %all-gather.6.cloned.1.call-update) | async-done | bytes 8388624 | tf_op jit(solution)/shard_map/all_gather | solution.py:119
  198.2 5.0 %fusion.20 = bf16[128,1024]{1,0:T(8,128)(2,1)S(1)} fusion(bf16[128,4096]{0,1:T(8,128)(2,1)} %all-gather.4.cloned.1.call-done, bf16[4096,1024]{1,0:T(8,128)(2,1)} %all-gather.6.cloned.1.call-done, bf16[128,1024]{1,0:T(8,128)(2,1)S(1)} %copy-done.3), kind=kOutput, calls=%fused_computation.26 | convolution fusion | flops 1074135040 | bytes 9961472 | tf_op jit(solution)/shard_map/dot_general | solution.py:117
  203.7 7.1 %all-reduce = (f32[128,16]{0,1:T(8,128)S(1)}, f32[128]{0:T(128)S(1)}) all-reduce(f32[128,16]{0,1:T(8,128)S(1)} %fusion.30, f32[128]{0:T(128)S(1)} %fusion.31), channel_id=1, replica_groups=mesh['grp'=2,'ep'=4,'tp'=4] {'tp'}, use_global_device_ids=true, to_apply=%region_3.4 | all-reduce | flops 2176 | bytes 17408 | tf_op jit(solution)/shard_map/psum | solution.py:124
  211.0 4.1 gather_fusion.2
  215.3 49.7 %all_to_all.16 = bf16[4,256,1024]{2,1,0:T(8,128)(2,1)S(1)} all-to-all(bf16[4,256,1024]{2,1,0:T(8,128)(2,1)S(1)} %broadcast_select_fusion), channel_id=1, replica_groups=mesh['grp'=2,'ep'=4,'tp'=4] {'ep'}, dimensions={0} | all-to-all | bytes 4194304 | tf_op jit(solution)/shard_map/all_to_all | solution.py:154
  265.0 13.6 %convert_bitcast_fusion = bf16[1024,4,2,4,64]{0,4,2,3,1:T(8,128)(2,1)} fusion(bf16[4,1024,2,1024,1]{3,2,1,0,4:T(2,128)(2,1)} %bitcast.169, bf16[4,4,64,1024,1]{3,2,1,0,4:T(8,128)(2,1)S(1)} %bitcast.156), kind=kOutput, calls=%fused_computation.10 | convolution fusion | flops 4297064448 | bytes 23068672 | tf_op jit(solution)/shard_map/secd,edgh->hegsc/dot_general | solution.py:159
  278.6 4.8 %copy.111 = bf16[1024,4,2,4,64]{0,4,3,2,1:T(8,128)(2,1)} copy(bf16[1024,4,2,4,64]{0,4,2,3,1:T(8,128)(2,1)} %convert_bitcast_fusion) | data formatting | bytes 8388608 | tf_op jit(solution)/shard_map/convert_element_type | solution.py:161
  283.5 43.8 %reduce-scatter.2.cloned.1.call-done = bf16[256,4,2,256]{0,3,2,1:T(8,128)(2,1)} async-done(((bf16[1024,4,2,256]{0,3,2,1:T(8,128)(2,1)}), bf16[256,4,2,256]{0,3,2,1:T(8,128)(2,1)}) %reduce-scatter.2.cloned.1.call-update) | async-done | bytes 1048592 | tf_op jit(solution)/shard_map/reduce_scatter | solution.py:160
  327.3 1.4 convert_element_type.119
  328.7 1.1 fusion.28
  329.8 23.0 %all-gather.8.cloned.1.call-done = bf16[1024,4,256]{0,2,1:T(8,128)(2,1)} async-done(((bf16[256,4,256]{0,2,1:T(8,128)(2,1)}), bf16[1024,4,256]{0,2,1:T(8,128)(2,1)}) %all-gather.8.cloned.1.call-update) | async-done | bytes 2097168 | tf_op jit(solution)/shard_map/all_gather | solution.py:169
  352.8 6.4 %convert_bitcast_fusion.1 = bf16[4,4,64,1024]{3,2,0,1:T(8,128)(2,1)S(1)} fusion(bf16[1024,4,4,64]{0,3,2,1:T(8,128)(2,1)} %bitcast.170, bf16[4,1024,1024]{2,1,0:T(8,128)(2,1)} %param.26), kind=kOutput, calls=%fused_computation.18 | convolution fusion | flops 2148532224 | bytes 12582912 | tf_op jit(solution)/shard_map/hesc,ehd->secd/dot_general | solution.py:171
  359.2 1.6 copy.113
  360.7 4.6 %all-to-all-start.2 = ((bf16[4,4,64,1024]{3,2,1,0:T(8,128)(2,1)}), bf16[4,4,64,1024]{3,2,1,0:T(8,128)(2,1)S(1)}, u32[]{:S(2)}, u32[]{:S(2)}) async-start(bf16[4,4,64,1024]{3,2,1,0:T(8,128)(2,1)} %copy.113), calls=%async_computation.3 | async-start | bytes 4194304 | tf_op jit(solution)/shard_map/all_to_all | solution.py:177
  365.9 7.0 %gather_fusion.4 = f32[1024]{0:T(1024)S(1)} fusion(f32[128,16]{0,1:T(8,128)S(1)} %broadcast_multiply_fusion, s32[1024]{0:T(1024)S(1)} %reshape.475), kind=kCustom, calls=%fused_computation.4 | custom fusion | bytes 16384 | tf_op jit(solution)/shard_map/jit(take_along_axis)/gather | solution.py:138
  373.3 40.7 %all-to-all-done.2 = bf16[4,4,64,1024]{3,2,1,0:T(8,128)(2,1)S(1)} async-done(((bf16[4,4,64,1024]{3,2,1,0:T(8,128)(2,1)}), bf16[4,4,64,1024]{3,2,1,0:T(8,128)(2,1)S(1)}, u32[]{:S(2)}, u32[]{:S(2)}) %all-to-all-start.2) | async-done | bytes 2097184 | tf_op jit(solution)/shard_map/all_to_all | solution.py:177
  414.0 5.4 %gather_fusion.3 = bf16[1024,1024]{1,0:T(8,128)(2,1)} fusion(bf16[1024,1024]{1,0:T(8,128)(2,1)S(1)} %bitcast.153, s32[1024]{0:T(1024)S(1)} %broadcast_clamp_fusion), kind=kCustom, calls=%fused_computation.3 | custom fusion | bytes 4198400 | tf_op jit(solution)/shard_map/jit(_take)/gather | solution.py:180
  419.3 2.4 fusion.8
  421.7 0.8 fusion.34
  (102 shorter events, 10.1 us)
Async XLA Ops:
  6.5 1.0 copy-start
  6.5 15.9 %copy-start.4 = (bf16[128,8,128]{2,1,0:T(8,128)(2,1)S(1)}, bf16[128,8,128]{2,1,0:T(8,128)(2,1)}, u32[]{:S(2)}) copy-start(bf16[128,8,128]{2,1,0:T(8,128)(2,1)} %param.15) | copy-start | bytes 786436
  6.5 15.9 %copy-start.2 = (s32[8]{0:T(128)S(1)}, s32[8]{0:T(128)}, u32[]{:S(2)}) copy-start(s32[8]{0:T(128)} %param.18) | copy-start | bytes 100
  9.7 15.3 %all-to-all-start = ((bf16[4,128,256]{2,1,0:T(8,128)(2,1)}), bf16[4,128,256]{2,1,0:T(8,128)(2,1)S(1)}, u32[]{:S(2)}, u32[]{:S(2)}) async-start(bf16[4,128,256]{2,1,0:T(8,128)(2,1)} %copy.90), calls=%async_computation | async-start | bytes 524288 | tf_op jit(solution)/shard_map/all_to_all | solution.py:48
  16.1 30.9 %all-gather.4.cloned.1.call-start = ((), (), s32[]{:S(2)}) async-start(), calls=%async_computation.4 | async-start | bytes 1310720 | tf_op jit(solution)/shard_map/all_gather | solution.py:115
  28.0 2.4 copy-start.5
  28.0 2.6 copy-start.7
  29.5 168.7 %copy-start.3 = (bf16[128,1024]{1,0:T(8,128)(2,1)S(1)}, bf16[128,1024]{1,0:T(8,128)(2,1)}, u32[]{:S(2)}) copy-start(bf16[128,1024]{1,0:T(8,128)(2,1)} %param.21) | copy-start | bytes 786436
  29.5 168.7 %all-gather.6.cloned.1.call-start = ((), (), s32[]{:S(2)}) async-start(), calls=%async_computation.5 | async-start | bytes 10485760 | tf_op jit(solution)/shard_map/all_gather | solution.py:119
  30.3 297.0 %reduce-scatter.2.cloned.1.call-start = ((), (), s32[]{:S(2)}) async-start(), calls=%async_computation.6 | async-start | bytes 5242880 | tf_op jit(solution)/shard_map/reduce_scatter | solution.py:160
  40.2 163.1 %copy-start.6 = (bf16[1024,16]{0,1:T(8,128)(2,1)S(1)}, bf16[1024,16]{0,1:T(8,128)(2,1)}, u32[]{:S(2)}) copy-start(bf16[1024,16]{0,1:T(8,128)(2,1)} %param.24) | copy-start | bytes 98308
  283.5 69.4 %all-gather.8.cloned.1.call-start = ((), (), s32[]{:S(2)}) async-start(), calls=%async_computation.7 | async-start | bytes 2621440 | tf_op jit(solution)/shard_map/all_gather | solution.py:169
  360.7 53.2 %all-to-all-start.2 = ((bf16[4,4,64,1024]{3,2,1,0:T(8,128)(2,1)}), bf16[4,4,64,1024]{3,2,1,0:T(8,128)(2,1)S(1)}, u32[]{:S(2)}, u32[]{:S(2)}) async-start(bf16[4,4,64,1024]{3,2,1,0:T(8,128)(2,1)} %copy.113), calls=%async_computation.3 | async-start | bytes 4194304 | tf_op jit(solution)/shard_map/all_to_all | solution.py:177
  414.0 8.6 %copy-start.1 = (bf16[2,128,4,2,128]{4,3,2,1,0:T(2,128)(2,1)S(1)}, bf16[2,128,4,2,128]{4,3,2,1,0:T(2,128)(2,1)}, u32[]{:S(2)}) copy-start(bf16[2,128,4,2,128]{4,3,2,1,0:T(2,128)(2,1)} %param.17) | copy-start | bytes 1572868
Sparse Core Ops, SparseCore 0:
  29.7 17.2 all-gather.3
  48.6 149.6 all-gather.5
  283.6 43.6 reduce-scatter.1
  330.0 22.8 all-gather.7
where the time goes:
time: 430 us; the launch traced here: 429 us
  waiting for transfers between devices  267 us (62%)
  blocking collectives  56.8 us (13%)
  local copies, waits for them, and re-layouts  34.9 us (8%)
  matrix products  30.2 us (7%)
  other arithmetic  15.4 us (4%)
  between operations  13.7 us (3%)
  starting transfers between devices  11.1 us (3%)
    all_gather x1, waiting for transfers between devices, per_device(): lax.all_gather(out_proj, 'ep', axis=0, tiled=True)  151 us
    all_to_all x1, blocking collectives, per_device(): lax.all_to_all(sending, 'ep', split_axis=0, concat_axis=0, tiled=True)  49.7 us
    reduce_scatter x1, waiting for transfers between devices, per_device(): lax.psum_scatter(term.reshape(lax.axis_size('tp') * hidden_here, local_ex...  43.8 us
    all_to_all x1, waiting for transfers between devices, per_device(): lax.all_to_all(expert_out.astype(jnp.bfloat16), 'ep', split_axis=0, conca...  40.7 us
    all_gather x1, waiting for transfers between devices, per_device(): piece = lax.all_gather(activated, 'tp', axis=0, tiled=True)  23 us
    dot_general x1, matrix products, per_device(): jnp.einsum('secd,edgh->hegsc', arrived, piece, preferred_element_type=jnp...  13.6 us
  transfers between devices with their start and end apart: 6, of which 6 were waited for; matrix products, arithmetic and copies ran while one was open for 6% of the time, Pallas kernels for 0%

commit v1 on v0

--- a/solution.py
+++ b/solution.py
@@ -58,6 +58,25 @@
         docs_per * doc_max
     )
     return (keys, values, valid)
+
+
+def project(attended, out_proj):
+    lanes = lax.axis_size("tp")
+    groups = lax.axis_size("ep")
+    length = attended.shape[0]
+    if lanes == groups:
+        swap = [(e * lanes + t, t * lanes + e) for e in range(groups) for t in range(lanes)]
+        block = lax.ppermute(attended, ("ep", "tp"), swap)
+        tokens = lax.all_gather(block, "tp", axis=0, tiled=True)
+    else:
+        all_heads = lax.all_gather(attended, "tp", axis=1, tiled=True)
+        split = jnp.swapaxes(all_heads.reshape(length, groups, -1), 0, 1)
+        tokens = lax.all_to_all(split, "ep", split_axis=0, concat_axis=0, tiled=True)
+        tokens = tokens.reshape(groups * length, -1)
+    part = jnp.dot(tokens, out_proj, preferred_element_type=jnp.float32)
+    return lax.psum_scatter(
+        part.astype(jnp.bfloat16), "ep", scatter_dimension=0, tiled=True
+    ).astype(jnp.float32)
 
 
 def per_device(
@@ -112,13 +131,8 @@
         .reshape(length, heads_here * head_dim)
         .astype(jnp.bfloat16)
     )
-    all_heads = lax.all_gather(attended, "tp", axis=1, tiled=True)
     width_here = hidden.shape[1]
-    projected = jnp.dot(
-        all_heads,
-        lax.all_gather(out_proj, "ep", axis=0, tiled=True),
-        preferred_element_type=jnp.float32,
-    )
+    projected = project(attended, out_proj)
     residual_wide = narrow(hidden.astype(jnp.float32) + projected).astype(jnp.float32)
     gain = norm_gain.astype(jnp.float32)
     squares, logit_part = lax.psum(
@@ -137,49 +151,57 @@
     logits = logit_part * inv_rms[:, None]
     mix = jax.nn.softmax(jnp.take_along_axis(logits, expert_ids, axis=1), axis=1)
     local_experts = w_gate_up.shape[0]
-    experts = local_experts * groups
-    choose = expert_ids.shape[1]
-    slots = length * choose
-    capacity = slots // experts
-    flat_ids = expert_ids.reshape(slots)
-    onehot = (flat_ids[:, None] == jnp.arange(experts, dtype=jnp.int32)[None, :]).astype(jnp.int32)
-    rank = jnp.sum(jnp.cumsum(onehot, axis=0) * onehot, axis=1) - 1
-    position = flat_ids * capacity + rank
-    source_row = (
-        jnp.zeros((slots,), jnp.int32)
-        .at[position]
-        .set(jnp.arange(slots, dtype=jnp.int32) // choose)
-    )
-    sending = jnp.take(normed, source_row, axis=0)
-    arrived = lax.all_to_all(sending, "ep", split_axis=0, concat_axis=0, tiled=True).reshape(
-        groups, local_experts, capacity, width_here
-    )
+    capacity = length * expert_ids.shape[1] // (local_experts * groups)
+    ids_all = lax.all_gather(expert_ids, "ep", axis=0)
+    local = device * local_experts + jnp.arange(local_experts, dtype=jnp.int32)
+    names = ids_all[:, :, :, None] == local
+    member = jnp.any(names, axis=2)
+    earlier = jnp.arange(length)[:, None] > jnp.arange(length)[None, :]
+    rank = jnp.einsum(
+        "nm,sme->sen",
+        earlier.astype(jnp.bfloat16),
+        member.astype(jnp.bfloat16),
+        preferred_element_type=jnp.float32,
+    )
+    seat = jnp.where(jnp.swapaxes(member, 1, 2), rank.astype(jnp.int32), -1)
+    picks = (seat[:, :, None, :] == jnp.arange(capacity, dtype=jnp.int32)[:, None]).astype(
+        jnp.bfloat16
+    )
+    normed_all = lax.all_gather(normed, "ep", axis=0)
+    mix_all = lax.all_gather(mix, "ep", axis=0)
+    share = jnp.sum(jnp.where(names, mix_all[:, :, :, None], 0.0), axis=2)
+    share = jnp.swapaxes(share, 1, 2)
+    arrived = jnp.einsum(
+        "secn,snd->escd", picks, normed_all, preferred_element_type=jnp.float32
+    ).astype(jnp.bfloat16)
+    rows = groups * capacity
+    arrived = arrived.reshape(local_experts, rows, width_here)
     hidden_here = HID // lanes
-    piece = w_gate_up
-    term = jnp.einsum("secd,edgh->hegsc", arrived, piece, preferred_element_type=jnp.float32)
+    term = jnp.einsum("erd,edgh->hegr", arrived, w_gate_up, preferred_element_type=jnp.float32)
     summed = lax.psum_scatter(
-        term.reshape(lax.axis_size("tp") * hidden_here, local_experts, 2, groups * capacity).astype(
-            jnp.bfloat16
-        ),
-        "tp",
-        scatter_dimension=0,
-        tiled=True,
+        term.astype(jnp.bfloat16), "tp", scatter_dimension=0, tiled=True
     ).astype(jnp.float32)
     activated = (jax.nn.silu(summed[:, :, 0]) * summed[:, :, 1]).astype(jnp.bfloat16)
     piece = lax.all_gather(activated, "tp", axis=0, tiled=True)
-    count = piece.shape[0]
     expert_out = jnp.einsum(
-        "hesc,ehd->secd",
-        piece.reshape(count, local_experts, groups, capacity),
-        w_down,
+        "her,ehd->erd", piece, w_down, preferred_element_type=jnp.float32
+    ).astype(jnp.bfloat16)
+    share_high = share.astype(jnp.bfloat16)
+    share_low = (share - share_high.astype(jnp.float32)).astype(jnp.bfloat16)
+    weights = jnp.stack([picks * share_high[:, :, None, :], picks * share_low[:, :, None, :]])
+    partial = jnp.einsum(
+        "psecn,escd->snd",
+        weights,
+        expert_out.reshape(local_experts, groups, capacity, width_here),
         preferred_element_type=jnp.float32,
     )
-    returned = lax.all_to_all(
-        expert_out.astype(jnp.bfloat16), "ep", split_axis=0, concat_axis=0, tiled=True
-    ).reshape(slots, width_here)
-    gathered = jnp.take(returned, position, axis=0).reshape(length, choose, width_here)
-    combined = jnp.einsum("tk,tkd->td", mix, gathered.astype(jnp.float32))
-    return (residual_wide + combined).astype(jnp.bfloat16)
+    combined = lax.psum_scatter(
+        partial.astype(jnp.bfloat16).reshape(groups * length, width_here),
+        "ep",
+        scatter_dimension=0,
+        tiled=True,
+    )
+    return (residual_wide + combined.astype(jnp.float32)).astype(jnp.bfloat16)
 
 
 def solution(mesh):

time: 430 us -> 262 us (0.61)
  waiting for transfers between devices: 267 us -> 146 us
  blocking collectives: 56.8 us -> 33.4 us
  local copies, waits for them, and re-layouts: 34.9 us -> 15.8 us
    all_gather x2, waiting for transfers between devices: 158 us -> 45.1 us  [the longest x1 32.5 us: project(): tokens = lax.all_gather(block, 'tp', axis=0, tiled=True)]
    reduce_scatter x1 -> x3, waiting for transfers between devices: 43.8 us -> 98.7 us  [the longest x1 43.9 us: per_device(): lax.psum_scatter(term.astype(jnp.bfloat16), 'tp', scatter_dimension=0, ti...]
    all_to_all x1 -> x0, blocking collectives: 49.7 us -> none  [per_device(): lax.all_to_all(sending, 'ep', split_axis=0, concat_axis=0, tiled=True)]
    all_to_all x1 -> x0, waiting for transfers between devices: 40.7 us -> none  [per_device(): lax.all_to_all(expert_out.astype(jnp.bfloat16), 'ep', split_axis=0, conca...]
    all_gather x0 -> x2, blocking collectives: none -> 26.9 us  [the longest x1 13.7 us: per_device(): ids_all = lax.all_gather(expert_ids, 'ep', axis=0)]
    all_gather x1, waiting for transfers between devices: 23 us -> 1.85 us  [per_device(): piece = lax.all_gather(activated, 'tp', axis=0, tiled=True)]
    gather x2 -> x0, local copies, waits for them, and re-layouts: 9.42 us -> none  [the longest x1 5.35 us: per_device(): jnp.take(returned, position, axis=0).reshape(length, choose, width_here)]
    convert_element_type x2 -> x1, local copies, waits for them, and re-layouts: 6.39 us -> 1.49 us  [per_device(): arrived = jnp.einsum('secn,snd->escd', picks, normed_all, preferred_eleme...]
  transfers between devices with their start and end apart: 6 -> 8, of which waited for: 6 -> 7; matrix products, arithmetic and copies ran while one was open for 6% -> 6% of each run, Pallas kernels for 0% -> 0%
where the time goes in v1:
time: 262 us; the launch traced here: 261 us
  waiting for transfers between devices  146 us (56%)
  blocking collectives  33.4 us (13%)
  matrix products  30.5 us (12%)
  local copies, waits for them, and re-layouts  15.8 us (6%)
  other arithmetic  14.2 us (5%)
  between operations  13.9 us (5%)
  starting transfers between devices  7.23 us (3%)
    reduce_scatter x1, waiting for transfers between devices, per_device(): lax.psum_scatter(term.astype(jnp.bfloat16), 'tp', scatter_dimension=0, ti...  43.9 us
    all_gather x1, waiting for transfers between devices, project(): tokens = lax.all_gather(block, 'tp', axis=0, tiled=True)  32.5 us
    reduce_scatter x1, waiting for transfers between devices, per_device(): lax.psum_scatter(partial.astype(jnp.bfloat16).reshape(groups * length, wi...  27.4 us
    reduce_scatter x1, waiting for transfers between devices, project(): lax.psum_scatter(part.astype(jnp.bfloat16), 'ep', scatter_dimension=0, ti...  27.4 us
    dot_general x1, matrix products, per_device(): jnp.einsum('erd,edgh->hegr', arrived, w_gate_up, preferred_element_type=j...  14.1 us
    all_gather x1, blocking collectives, per_device(): ids_all = lax.all_gather(expert_ids, 'ep', axis=0)  13.7 us
    all_gather x1, blocking collectives, per_device(): mix_all = lax.all_gather(mix, 'ep', axis=0)  13.3 us
    all_gather x1, waiting for transfers between devices, per_device(): normed_all = lax.all_gather(normed, 'ep', axis=0)  12.6 us
  transfers between devices with their start and end apart: 8, of which 7 were waited for; matrix products, arithmetic and copies ran while one was open for 6% of the time, Pallas kernels for 0%

profile of v1, /device:TPU:0, one launch (start us, length us, event | category | flops | bytes accessed | tf_op | source)
XLA Modules:
  0.0 260.9 jit_solution(11655026482860830586)
XLA Ops:
  6.5 1.1 constant_dynamic-slice_fusion.2
  7.8 0.8 convert_reduce_fusion.1
  9.0 0.7 copy.76
  9.7 6.3 %all-to-all-start = ((bf16[4,128,256]{2,1,0:T(8,128)(2,1)}), bf16[4,128,256]{2,1,0:T(8,128)(2,1)S(1)}, u32[]{:S(2)}, u32[]{:S(2)}) async-start(bf16[4,128,256]{2,1,0:T(8,128)(2,1)} %copy.76), calls=%async_computation | async-start | bytes 524288 | tf_op jit(solution)/shard_map/all_to_all | solution.py:48
  16.1 0.7 fusion.66
  18.2 2.7 %compare_select_fusion.3 = s32[512,1]{0,1:T(1,128)S(1)} fusion(s32[512,1]{0,1:T(1,128)S(1)} %bitcast.156, s32[512,1]{0,1:T(1,128)S(1)} %bitcast.157, s32[]{:T(128)} %bitcast.11, s32[]{:T(128)} %bitcast.12, s32[]{:T(128)} %bitcast.14, s32[]{:T(128)} %bitcast.13), kind=kLoop, calls=%fused_computation.95 | loop fusion | flops 4096 | bytes 6160 | tf_op jit(solution)/shard_map/jit(_take)/gather | solution.py:52
  20.9 0.9 constant_dynamic-slice_fusion
  23.9 0.9 subtract_convert_fusion
  26.8 1.6 fusion.8
  28.9 0.8 fusion.20
  30.5 0.7 copy-done.4
  31.3 32.5 %all-gather.7.cloned.1.call-done = bf16[512,1024]{0,1:T(8,128)(2,1)} async-done(((bf16[128,1024]{0,1:T(8,128)(2,1)}), bf16[512,1024]{0,1:T(8,128)(2,1)}) %all-gather.7.cloned.1.call-update) | async-done | bytes 1048592 | tf_op jit(solution)/shard_map/all_gather | solution.py:70
  63.8 3.5 %convolution_convert_fusion.1 = bf16[512,1024]{1,0:T(8,128)(2,1)} fusion(bf16[512,1024]{0,1:T(8,128)(2,1)} %all-gather.7.cloned.1.call-done, bf16[1024,1024]{1,0:T(8,128)(2,1)S(1)} %copy-done), kind=kOutput, calls=%fused_computation.16 | convolution fusion | flops 1074266112 | bytes 4194304 | tf_op jit(solution)/shard_map/dot_general | solution.py:76
  67.3 27.4 %reduce-scatter.4.cloned.1.call-done = bf16[128,1024]{1,0:T(8,128)(2,1)} async-done(((bf16[512,1024]{1,0:T(8,128)(2,1)}), bf16[128,1024]{1,0:T(8,128)(2,1)}) %reduce-scatter.4.cloned.1.call-update) | async-done | bytes 262160 | tf_op jit(solution)/shard_map/reduce_scatter | solution.py:77
  94.7 1.0 add_convert_fusion
  96.2 6.4 %all-reduce = (f32[128,16]{0,1:T(8,128)S(1)}, f32[128]{0:T(128)S(1)}) all-reduce(f32[128,16]{0,1:T(8,128)S(1)} %fusion.26, f32[128]{0:T(128)S(1)} %fusion.27), channel_id=1, replica_groups=mesh['grp'=2,'ep'=4,'tp'=4] {'tp'}, use_global_device_ids=true, to_apply=%region_5.6 | all-reduce | flops 2176 | bytes 17408 | tf_op jit(solution)/shard_map/psum | solution.py:138
  102.7 0.8 fusion.29
  103.6 13.7 %all-gather = s32[512,8]{0,1:T(8,128)S(1)} all-gather(s32[128,8]{0,1:T(8,128)S(1)} %copy-done.5), channel_id=2, replica_groups=mesh['grp'=2,'ep'=4,'tp'=4] {'ep'}, dimensions={0}, use_global_device_ids=true | all-gather | bytes 20480 | tf_op jit(solution)/shard_map/all_gather | solution.py:155
  117.5 12.6 %all-gather.11.cloned.1.call-done = bf16[512,1024]{1,0:T(8,128)(2,1)} async-done(((bf16[128,1024]{1,0:T(8,128)(2,1)}), bf16[512,1024]{1,0:T(8,128)(2,1)}) %all-gather.11.cloned.1.call-update) | async-done | bytes 1048592 | tf_op jit(solution)/shard_map/all_gather | solution.py:170
  130.1 1.9 convert_bitcast_fusion.1
  132.0 1.5 copy.88
  133.5 14.1 %convert_bitcast_fusion = bf16[1024,4,2,256]{0,3,2,1:T(8,128)(2,1)} fusion(bf16[4,256,1024,1]{2,1,3,0:T(8,128)(2,1)} %bitcast.148, bf16[4,1024,2,1024]{3,2,1,0:T(2,128)(2,1)} %param.25), kind=kOutput, calls=%fused_computation.5 | convolution fusion | flops 4297064448 | bytes 23068672 | tf_op jit(solution)/shard_map/erd,edgh->hegr/dot_general | solution.py:180
  147.7 43.9 %reduce-scatter.6.cloned.1.call-done = bf16[256,4,2,256]{0,3,2,1:T(8,128)(2,1)} async-done(((bf16[1024,4,2,256]{0,3,2,1:T(8,128)(2,1)}), bf16[256,4,2,256]{0,3,2,1:T(8,128)(2,1)}) %reduce-scatter.6.cloned.1.call-update) | async-done | bytes 1048592 | tf_op jit(solution)/shard_map/reduce_scatter | solution.py:181
  191.6 1.4 convert_element_type.150
  193.0 1.1 fusion.25
  194.3 7.0 %gather_fusion.2 = f32[1024]{0:T(1024)S(1)} fusion(f32[128,16]{0,1:T(8,128)S(1)} %broadcast_multiply_fusion, s32[1024]{0:T(1024)S(1)} %reshape.416), kind=kCustom, calls=%fused_computation.2 | custom fusion | bytes 16384 | tf_op jit(solution)/shard_map/jit(take_along_axis)/gather | solution.py:152
  201.6 13.3 %all-gather.1 = f32[512,8]{0,1:T(8,128)S(1)} all-gather(f32[128,8]{0,1:T(8,128)S(1)} %fusion.61), channel_id=3, replica_groups=mesh['grp'=2,'ep'=4,'tp'=4] {'ep'}, dimensions={0}, use_global_device_ids=true | all-gather | bytes 20480 | tf_op jit(solution)/shard_map/all_gather | solution.py:171
  215.2 1.9 all-gather.9.cloned.1.call-done
  217.0 6.4 %convolution_convert_fusion = bf16[4,256,1024]{2,1,0:T(8,128)(2,1)S(1)} fusion(bf16[1024,4,256]{0,2,1:T(8,128)(2,1)} %all-gather.9.cloned.1.call-done, bf16[4,1024,1024]{2,1,0:T(8,128)(2,1)} %param.26), kind=kOutput, calls=%fused_computation.15 | convolution fusion | flops 2148532224 | bytes 12582912 | tf_op jit(solution)/shard_map/her,ehd->erd/dot_general | solution.py:186
  223.4 1.5 bitcast_convert_fusion
  224.9 27.4 %reduce-scatter.8.cloned.1.call-done = bf16[128,1024]{1,0:T(8,128)(2,1)} async-done(((bf16[512,1024]{1,0:T(8,128)(2,1)}), bf16[128,1024]{1,0:T(8,128)(2,1)}) %reduce-scatter.8.cloned.1.call-update) | async-done | bytes 262160 | tf_op jit(solution)/shard_map/reduce_scatter | solution.py:198
  252.3 1.7 fusion.30
  (86 shorter events, 8.9 us)
Async XLA Ops:
  6.5 57.2 %copy-start = (bf16[1024,1024]{1,0:T(8,128)(2,1)S(1)}, bf16[1024,1024]{1,0:T(8,128)(2,1)}, u32[]{:S(2)}) copy-start(bf16[1024,1024]{1,0:T(8,128)(2,1)} %param.22) | copy-start | bytes 6291460
  6.5 15.9 %copy-start.2 = (bf16[128,8,128]{2,1,0:T(8,128)(2,1)S(1)}, bf16[128,8,128]{2,1,0:T(8,128)(2,1)}, u32[]{:S(2)}) copy-start(bf16[128,8,128]{2,1,0:T(8,128)(2,1)} %param.15) | copy-start | bytes 786436
  6.5 16.0 %copy-start.1 = (s32[8]{0:T(128)S(1)}, s32[8]{0:T(128)}, u32[]{:S(2)}) copy-start(s32[8]{0:T(128)} %param.18) | copy-start | bytes 100
  9.7 15.3 %all-to-all-start = ((bf16[4,128,256]{2,1,0:T(8,128)(2,1)}), bf16[4,128,256]{2,1,0:T(8,128)(2,1)S(1)}, u32[]{:S(2)}, u32[]{:S(2)}) async-start(bf16[4,128,256]{2,1,0:T(8,128)(2,1)} %copy.76), calls=%async_computation | async-start | bytes 524288 | tf_op jit(solution)/shard_map/all_to_all | solution.py:48
  16.1 47.7 %all-gather.7.cloned.1.call-start = ((), (), s32[]{:S(2)}) async-start(), calls=%async_computation.4 | async-start | bytes 1310720 | tf_op jit(solution)/shard_map/all_gather | solution.py:70
  29.7 0.7 collective-permute-start
  30.4 0.7 copy-start.4
  31.2 36.1 %copy-start.7 = (bf16[1024]{0:T(1024)(128)(2,1)S(1)}, bf16[1024]{0:T(1024)(128)(2,1)}, u32[]{:S(2)}) copy-start(bf16[1024]{0:T(1024)(128)(2,1)} %param.23) | copy-start | bytes 6148
  31.2 63.5 %copy-start.3 = (bf16[128,1024]{1,0:T(8,128)(2,1)S(1)}, bf16[128,1024]{1,0:T(8,128)(2,1)}, u32[]{:S(2)}) copy-start(bf16[128,1024]{1,0:T(8,128)(2,1)} %param.21) | copy-start | bytes 786436
  31.2 64.7 %copy-start.6 = (bf16[1024,16]{0,1:T(8,128)(2,1)S(1)}, bf16[1024,16]{0,1:T(8,128)(2,1)}, u32[]{:S(2)}) copy-start(bf16[1024,16]{0,1:T(8,128)(2,1)} %param.24) | copy-start | bytes 98308
  31.2 63.5 %reduce-scatter.4.cloned.1.call-start = ((), (), s32[]{:S(2)}) async-start(), calls=%async_computation.5 | async-start | bytes 1310720 | tf_op jit(solution)/shard_map/reduce_scatter | solution.py:77
  67.2 36.4 %copy-start.5 = (s32[128,8]{0,1:T(8,128)S(1)}, s32[128,8]{0,1:T(8,128)}, u32[]{:S(2)}) copy-start(s32[128,8]{0,1:T(8,128)} %param.27) | copy-start | bytes 12292
  67.3 62.8 %all-gather.11.cloned.1.call-start = ((), (), s32[]{:S(2)}) async-start(), calls=%async_computation.9 | async-start | bytes 1310720 | tf_op jit(solution)/shard_map/all_gather | solution.py:170
  103.5 88.0 %reduce-scatter.6.cloned.1.call-start = ((), (), s32[]{:S(2)}) async-start(), calls=%async_computation.6 | async-start | bytes 5242880 | tf_op jit(solution)/shard_map/reduce_scatter | solution.py:181
  147.6 69.4 %all-gather.9.cloned.1.call-start = ((), (), s32[]{:S(2)}) async-start(), calls=%async_computation.7 | async-start | bytes 2621440 | tf_op jit(solution)/shard_map/all_gather | solution.py:185
  194.1 58.3 %reduce-scatter.8.cloned.1.call-start = ((), (), s32[]{:S(2)}) async-start(), calls=%async_computation.8 | async-start | bytes 1310720 | tf_op jit(solution)/shard_map/reduce_scatter | solution.py:198
Sparse Core Ops, SparseCore 0:
  31.3 32.4 all-gather.6
  67.4 27.2 reduce-scatter.3
  103.7 26.3 all-gather.10
  147.8 43.7 reduce-scatter.5
  194.2 22.7 all-gather.8
  225.0 27.2 reduce-scatter.7

commit v2 on v1

--- a/solution.py
+++ b/solution.py
@@ -3,6 +3,8 @@
 import jax
 import jax.numpy as jnp
 from jax import lax
+from jax.experimental import pallas as pl
+from jax.experimental.pallas import tpu as pltpu
 from jax.sharding import PartitionSpec as P
 
 D = 4096
@@ -77,6 +79,156 @@
     return lax.psum_scatter(
         part.astype(jnp.bfloat16), "ep", scatter_dimension=0, tiled=True
     ).astype(jnp.float32)
+
+
+def expert_kernel(
+    tokens, w_in_hbm, w_out_hbm, result,
+    w_in, w_out, sent, first, pair, second, acts,
+    load_in, load_out, send_sem, recv_sem,
+):
+    count, rows, _ = tokens.shape
+    lane = lax.axis_index("tp")
+    chip = lane // 2
+    core = lane % 2
+    partner = chip * 2 + (1 - core)
+    across = (1 - chip) * 2 + core
+    loads_in = [
+        pltpu.make_async_copy(w_in_hbm.at[e], w_in.at[e], load_in.at[e]) for e in range(count)
+    ]
+    loads_out = [
+        pltpu.make_async_copy(w_out_hbm.at[e], w_out.at[e], load_out.at[e]) for e in range(count)
+    ]
+    for load in loads_in + loads_out:
+        load.start()
+    barrier = pltpu.get_barrier_semaphore()
+    for other in (partner, across):
+        pl.semaphore_signal(
+            barrier, inc=1, device_id={"tp": other}, device_id_type=pl.DeviceIdType.MESH
+        )
+    pl.semaphore_wait(barrier, 2)
+
+    def remote(kind, e, source, target, other):
+        return pltpu.make_async_remote_copy(
+            src_ref=source,
+            dst_ref=target,
+            send_sem=send_sem.at[kind, e],
+            recv_sem=recv_sem.at[kind, e],
+            device_id={"tp": other},
+            device_id_type=pl.DeviceIdType.MESH,
+        )
+
+    copies = [
+        [
+            remote(0, e, sent.at[e, 1 - core], first.at[e], partner),
+            remote(1, e, pair.at[e], second.at[e], across),
+            remote(2, e, acts.at[e, core, chip], acts.at[e, core, chip], across),
+            remote(3, e, acts.at[e, core, chip], acts.at[e, core, chip], partner),
+            remote(4, e, acts.at[e, core, 1 - chip], acts.at[e, core, 1 - chip], partner),
+        ]
+        for e in range(count)
+    ]
+
+    def multiply_in(e):
+        loads_in[e].wait()
+
+        def block(i, carry):
+            part = jnp.dot(
+                tokens[e], w_in[e, i // 2, i % 2], preferred_element_type=jnp.float32
+            )
+            sent[e, i // 2, i % 2] = part.astype(jnp.bfloat16)
+            return carry
+
+        lax.fori_loop(0, 4, block, 0)
+        copies[e][0].start()
+
+    def add_pair(e):
+        copies[e][0].wait_recv()
+        total = sent[e, core, 1 - chip].astype(jnp.float32) + first[e, 1 - chip].astype(jnp.float32)
+        pair[e] = total.astype(jnp.bfloat16)
+        copies[e][1].start()
+
+    def activate(e):
+        copies[e][1].wait_recv()
+        total = (
+            sent[e, core, chip].astype(jnp.float32)
+            + first[e, chip].astype(jnp.float32)
+            + second[e].astype(jnp.float32)
+        )
+        half = total.shape[1] // 2
+        gate = total[:, :half]
+        acts[e, core, chip] = (gate / (1.0 + jnp.exp(-gate)) * total[:, half:]).astype(jnp.bfloat16)
+        copies[e][2].start()
+        copies[e][3].start()
+
+    def forward(e):
+        copies[e][2].wait_recv()
+        copies[e][4].start()
+
+    def multiply_out(e):
+        copies[e][3].wait_recv()
+        copies[e][4].wait_recv()
+        loads_out[e].wait()
+        joined = jnp.concatenate([acts[e, i % 2, i // 2] for i in range(4)], axis=1)
+        result[e] = jnp.dot(joined, w_out[e], preferred_element_type=jnp.float32).astype(
+            jnp.bfloat16
+        )
+
+    stages = (multiply_in, add_pair, activate, forward, multiply_out)
+    delays = (0, 1, 3, 4, 5)
+    for tick in range(count + delays[-1]):
+        for stage, delay in zip(stages, delays):
+            if 0 <= tick - delay < count:
+                stage(tick - delay)
+    for group in copies:
+        for copy in group:
+            copy.wait_send()
+
+
+def feed_forward(arrived, w_gate_up, w_down):
+    count, rows, width = arrived.shape
+    lanes = lax.axis_size("tp")
+    hidden_here = HID // lanes
+    if lanes == 4:
+        w_in = w_gate_up.reshape(count, width, 2, 2, 2, hidden_here)
+        w_in = jnp.transpose(w_in, (0, 4, 3, 1, 2, 5)).reshape(
+            count, 2, 2, width, 2 * hidden_here
+        )
+        bf16 = jnp.bfloat16
+        return pl.pallas_call(
+            expert_kernel,
+            out_shape=jax.ShapeDtypeStruct(arrived.shape, bf16),
+            in_specs=[
+                pl.BlockSpec(memory_space=pltpu.VMEM),
+                pl.BlockSpec(memory_space=pl.ANY),
+                pl.BlockSpec(memory_space=pl.ANY),
+            ],
+            out_specs=pl.BlockSpec(memory_space=pltpu.VMEM),
+            scratch_shapes=[
+                pltpu.VMEM(w_in.shape, bf16),
+                pltpu.VMEM(w_down.shape, bf16),
+                pltpu.VMEM((count, 2, 2, rows, 2 * hidden_here), bf16),
+                pltpu.VMEM((count, 2, rows, 2 * hidden_here), bf16),
+                pltpu.VMEM((count, rows, 2 * hidden_here), bf16),
+                pltpu.VMEM((count, rows, 2 * hidden_here), bf16),
+                pltpu.VMEM((count, 2, 2, rows, hidden_here), bf16),
+                pltpu.SemaphoreType.DMA((count,)),
+                pltpu.SemaphoreType.DMA((count,)),
+                pltpu.SemaphoreType.DMA((5, count)),
+                pltpu.SemaphoreType.DMA((5, count)),
+            ],
+            compiler_params=pltpu.CompilerParams(
+                collective_id=1, has_side_effects=True, vmem_limit_bytes=50 << 20
+            ),
+        )(arrived, w_in, w_down)
+    term = jnp.einsum("erd,edgh->hegr", arrived, w_gate_up, preferred_element_type=jnp.float32)
+    summed = lax.psum_scatter(
+        term.astype(jnp.bfloat16), "tp", scatter_dimension=0, tiled=True
+    ).astype(jnp.float32)
+    activated = (jax.nn.silu(summed[:, :, 0]) * summed[:, :, 1]).astype(jnp.bfloat16)
+    piece = lax.all_gather(activated, "tp", axis=0, tiled=True)
+    return jnp.einsum(
+        "her,ehd->erd", piece, w_down, preferred_element_type=jnp.float32
+    ).astype(jnp.bfloat16)
 
 
 def per_device(
@@ -149,13 +301,27 @@
     inv_rms = lax.rsqrt(squares / D + norm_eps)
     normed = (residual_wide * inv_rms[:, None] * gain[None, :]).astype(jnp.bfloat16)
     logits = logit_part * inv_rms[:, None]
-    mix = jax.nn.softmax(jnp.take_along_axis(logits, expert_ids, axis=1), axis=1)
     local_experts = w_gate_up.shape[0]
     capacity = length * expert_ids.shape[1] // (local_experts * groups)
-    ids_all = lax.all_gather(expert_ids, "ep", axis=0)
-    local = device * local_experts + jnp.arange(local_experts, dtype=jnp.int32)
-    names = ids_all[:, :, :, None] == local
-    member = jnp.any(names, axis=2)
+    experts = logits.shape[1]
+    chosen = jnp.any(expert_ids[:, :, None] == jnp.arange(experts, dtype=jnp.int32), axis=1)
+    top = jnp.max(jnp.where(chosen, logits, -jnp.inf), axis=1, keepdims=True)
+    raised = jnp.where(chosen, jnp.exp(jnp.where(chosen, logits - top, 0.0)), 0.0)
+    mix = raised / jnp.sum(raised, axis=1, keepdims=True)
+    mix_high = mix.astype(jnp.bfloat16)
+    mix_low = (mix - mix_high.astype(jnp.float32)).astype(jnp.bfloat16)
+    notes = jnp.concatenate([chosen.astype(jnp.bfloat16), mix_high, mix_low], axis=1)
+    notes = jnp.pad(notes, ((0, 0), (0, -notes.shape[1] % 128)))
+    packed = lax.all_gather(jnp.concatenate([normed, notes], axis=1), "ep", axis=0)
+    normed_all = packed[:, :, :width_here]
+
+    def mine(index):
+        start = width_here + index * experts + device * local_experts
+        return lax.dynamic_slice_in_dim(packed, start, local_experts, axis=2)
+
+    member = mine(0) > 0
+    share_high = jnp.swapaxes(mine(1), 1, 2)
+    share_low = jnp.swapaxes(mine(2), 1, 2)
     earlier = jnp.arange(length)[:, None] > jnp.arange(length)[None, :]
     rank = jnp.einsum(
         "nm,sme->sen",
@@ -167,27 +333,12 @@
     picks = (seat[:, :, None, :] == jnp.arange(capacity, dtype=jnp.int32)[:, None]).astype(
         jnp.bfloat16
     )
-    normed_all = lax.all_gather(normed, "ep", axis=0)
-    mix_all = lax.all_gather(mix, "ep", axis=0)
-    share = jnp.sum(jnp.where(names, mix_all[:, :, :, None], 0.0), axis=2)
-    share = jnp.swapaxes(share, 1, 2)
     arrived = jnp.einsum(
         "secn,snd->escd", picks, normed_all, preferred_element_type=jnp.float32
     ).astype(jnp.bfloat16)
     rows = groups * capacity
     arrived = arrived.reshape(local_experts, rows, width_here)
-    hidden_here = HID // lanes
-    term = jnp.einsum("erd,edgh->hegr", arrived, w_gate_up, preferred_element_type=jnp.float32)
-    summed = lax.psum_scatter(
-        term.astype(jnp.bfloat16), "tp", scatter_dimension=0, tiled=True
-    ).astype(jnp.float32)
-    activated = (jax.nn.silu(summed[:, :, 0]) * summed[:, :, 1]).astype(jnp.bfloat16)
-    piece = lax.all_gather(activated, "tp", axis=0, tiled=True)
-    expert_out = jnp.einsum(
-        "her,ehd->erd", piece, w_down, preferred_element_type=jnp.float32
-    ).astype(jnp.bfloat16)
-    share_high = share.astype(jnp.bfloat16)
-    share_low = (share - share_high.astype(jnp.float32)).astype(jnp.bfloat16)
+    expert_out = feed_forward(arrived, w_gate_up, w_down)
     weights = jnp.stack([picks * share_high[:, :, None, :], picks * share_low[:, :, None, :]])
     partial = jnp.einsum(
         "psecn,escd->snd",

time: 262 us -> 273 us (1.042)
  local copies, waits for them, and re-layouts: 15.8 us -> 90.3 us
  waiting for transfers between devices: 146 us -> 86.3 us
  Pallas kernels: 0 us -> 45.2 us
  blocking collectives: 33.4 us -> 6.43 us
  matrix products: 30.5 us -> 9.86 us
    reshape x0 -> x3, local copies, waits for them, and re-layouts: none -> 78.7 us  [the longest x2 51.7 us: feed_forward(): w_in = w_gate_up.reshape(count, width, 2, 2, 2, hidden_here)]
    pallas_call x0 -> x1, Pallas kernels: none -> 45.2 us  [feed_forward(): pl.pallas_call(expert_kernel, out_shape=jax.ShapeDtypeStruct(arrived.shap...]
    reduce_scatter x1 -> x0, waiting for transfers between devices: 43.9 us -> none  [per_device(): lax.psum_scatter(term.astype(jnp.bfloat16), 'tp', scatter_dimension=0, ti...]
    all_gather x2 -> x0, blocking collectives: 26.9 us -> none  [the longest x1 13.7 us: per_device(): ids_all = lax.all_gather(expert_ids, 'ep', axis=0)]
    dot_general x2 -> x0, matrix products: 20.5 us -> none  [the longest x1 14.1 us: per_device(): jnp.einsum('erd,edgh->hegr', arrived, w_gate_up, preferred_element_type=j...]
    all_gather x2 -> x1, waiting for transfers between devices: 14.4 us -> 0.01 us  [per_device(): lax.all_gather(jnp.concatenate([normed, notes], axis=1), 'ep', axis=0)]
    gather x5 -> x0, local copies, waits for them, and re-layouts: 7.34 us -> none  [per_device(): jnp.take_along_axis(logits, expert_ids, axis=1)]
  transfers between devices with their start and end apart: 8 -> 6, of which waited for: 7 -> 3; matrix products, arithmetic and copies ran while one was open for 6% -> 33% of each run, Pallas kernels for 0% -> 0%
where the time goes in v2:
time: 273 us; the launch traced here: 271 us
  local copies, waits for them, and re-layouts  90.3 us (33%)
  waiting for transfers between devices  86.3 us (32%)
  Pallas kernels  45.2 us (17%)
  between operations  13.6 us (5%)
  other arithmetic  12.2 us (4%)
  matrix products  9.86 us (4%)
  starting transfers between devices  7.33 us (3%)
  blocking collectives  6.43 us (2%)
    reshape x2, local copies, waits for them, and re-layouts, feed_forward(): w_in = w_gate_up.reshape(count, width, 2, 2, 2, hidden_here)  51.7 us
    pallas_call x1, Pallas kernels, feed_forward(): pl.pallas_call(expert_kernel, out_shape=jax.ShapeDtypeStruct(arrived.shap...  45.2 us
    all_gather x1, waiting for transfers between devices, project(): tokens = lax.all_gather(block, 'tp', axis=0, tiled=True)  32.7 us
    reduce_scatter x1, waiting for transfers between devices, project(): lax.psum_scatter(part.astype(jnp.bfloat16), 'ep', scatter_dimension=0, ti...  27.3 us
    reshape x1, local copies, waits for them, and re-layouts, feed_forward(): jnp.transpose(w_in, (0, 4, 3, 1, 2, 5))  26.9 us
    reduce_scatter x1, waiting for transfers between devices, per_device(): lax.psum_scatter(partial.astype(jnp.bfloat16).reshape(groups * length, wi...  26.2 us
    psum x1, blocking collectives, per_device(): lax.psum((jnp.sum(residual_wide * residual_wide, axis=1), jnp.dot(residua...  6.43 us
    all_to_all x1, starting transfers between devices, fetch_context(): lax.all_to_all(sending, 'ep', split_axis=0, concat_axis=0, tiled=True)  6.35 us
  transfers between devices with their start and end apart: 6, of which 3 were waited for; matrix products, arithmetic and copies ran while one was open for 33% of the time, Pallas kernels for 0%

profile of v2, /device:TPU:0, one launch (start us, length us, event | category | flops | bytes accessed | tf_op | source)
XLA Modules:
  0.0 271.2 jit_solution(11567435337089204618)
XLA Ops:
  6.6 1.2 constant_dynamic-slice_fusion.3
  7.8 0.8 convert_reduce_fusion.1
  9.0 0.7 copy.72
  9.7 6.3 %all-to-all-start = ((bf16[4,128,256]{2,1,0:T(8,128)(2,1)}), bf16[4,128,256]{2,1,0:T(8,128)(2,1)S(1)}, u32[]{:S(2)}, u32[]{:S(2)}) async-start(bf16[4,128,256]{2,1,0:T(8,128)(2,1)} %copy.72), calls=%async_computation | async-start | bytes 524288 | tf_op jit(solution)/shard_map/all_to_all | solution.py:50
  16.1 0.7 fusion.63
  16.8 0.7 constant_dynamic-slice_fusion.2
  18.2 2.6 compare_select_fusion.1
  22.1 0.9 constant_dynamic-slice_fusion.1
  23.4 0.8 subtract_convert_fusion.1
  24.2 0.7 copy.78
  24.9 0.7 copy.77
  25.6 1.1 subtract_convert_fusion
  28.6 1.3 fusion.4
  30.5 0.8 fusion.16
  31.3 0.7 collective-permute-start
  32.0 0.7 copy-done.5
  32.8 32.7 %all-gather.4.cloned.1.call-done = bf16[512,1024]{0,1:T(8,128)(2,1)} async-done(((bf16[128,1024]{0,1:T(8,128)(2,1)}), bf16[512,1024]{0,1:T(8,128)(2,1)}) %all-gather.4.cloned.1.call-update) | async-done | bytes 1048592 | tf_op jit(solution)/shard_map/all_gather | solution.py:72
  65.5 3.5 %convolution_convert_fusion = bf16[512,1024]{1,0:T(8,128)(2,1)} fusion(bf16[512,1024]{0,1:T(8,128)(2,1)} %all-gather.4.cloned.1.call-done, bf16[1024,1024]{1,0:T(8,128)(2,1)S(1)} %copy-done), kind=kOutput, calls=%fused_computation.12 | convolution fusion | flops 1074266112 | bytes 4194304 | tf_op jit(solution)/shard_map/dot_general | solution.py:78
  69.1 27.3 %reduce-scatter.3.cloned.1.call-done = bf16[128,1024]{1,0:T(8,128)(2,1)} async-done(((bf16[512,1024]{1,0:T(8,128)(2,1)}), bf16[128,1024]{1,0:T(8,128)(2,1)}) %reduce-scatter.3.cloned.1.call-update) | async-done | bytes 262160 | tf_op jit(solution)/shard_map/reduce_scatter | solution.py:79
  96.4 1.0 add_convert_fusion
  97.9 6.4 %all-reduce.1 = (f32[128,16]{0,1:T(8,128)S(1)}, f32[128]{0:T(128)S(1)}) all-reduce(f32[128,16]{0,1:T(8,128)S(1)} %fusion.24, f32[128]{0:T(128)S(1)} %fusion.21), channel_id=1, replica_groups=mesh['grp'=2,'ep'=4,'tp'=4] {'tp'}, use_global_device_ids=true, to_apply=%region_7.8 | all-reduce | flops 2176 | bytes 17408 | tf_op jit(solution)/shard_map/psum | solution.py:290
  104.7 0.8 fusion.28
  105.7 27.1 %reshape.359 = bf16[4,1024,2,2,2,256]{5,4,3,2,1,0:T(2,128)(2,1)} reshape(bf16[4,1024,2,1024]{3,2,1,0:T(2,128)(2,1)} %param.25) | data formatting | bytes 33554432 | tf_op jit(solution)/shard_map/reshape | solution.py:192
  132.8 24.7 %copy.106 = bf16[4,1024,2,2,2,256]{5,2,1,3,4,0:T(2,128)(2,1)} copy(bf16[4,1024,2,2,2,256]{5,4,3,2,1,0:T(2,128)(2,1)} %reshape.359) | data formatting | bytes 33554432 | tf_op jit(solution)/shard_map/reshape | solution.py:192
  157.5 26.9 %reshape.360.w_in_hbm = bf16[4,2,2,1024,512]{4,3,2,1,0:T(8,128)(2,1)} reshape(bf16[4,2,2,1024,2,256]{5,4,3,2,1,0:T(2,128)(2,1)} %bitcast.121) | data formatting | bytes 33554432 | tf_op jit(solution)/shard_map/reshape | solution.py:193
  184.4 1.4 dynamic-slice_bitcast_fusion.1
  186.3 1.9 convert_bitcast_fusion
  188.3 1.6 copy.86
  190.0 45.2 %shard_map.127 = bf16[4,256,1024]{2,1,0:T(8,128)(2,1)S(1)} custom-call(bf16[4,256,1024]{2,1,0:T(8,128)(2,1)} %bitcast.122, bf16[4,2,2,1024,512]{4,3,2,1,0:T(8,128)(2,1)} %reshape.360.w_in_hbm, bf16[4,1024,1024]{2,1,0:T(8,128)(2,1)} %w_out_hbm.1), custom_call_target="tpu_custom_call" | custom-call | tf_op jit(solution)/shard_map/pallas_call | solution.py:197
  235.3 1.5 bitcast_convert_fusion
  236.7 26.2 %reduce-scatter.5.cloned.1.call-done = bf16[128,1024]{1,0:T(8,128)(2,1)} async-done(((bf16[512,1024]{1,0:T(8,128)(2,1)}), bf16[128,1024]{1,0:T(8,128)(2,1)}) %reduce-scatter.5.cloned.1.call-update) | async-done | bytes 262160 | tf_op jit(solution)/shard_map/reduce_scatter | solution.py:349
  263.0 1.7 fusion.25
  (78 shorter events, 7.1 us)
Async XLA Ops:
  6.5 58.9 %copy-start = (bf16[1024,1024]{1,0:T(8,128)(2,1)S(1)}, bf16[1024,1024]{1,0:T(8,128)(2,1)}, u32[]{:S(2)}) copy-start(bf16[1024,1024]{1,0:T(8,128)(2,1)} %param.22) | copy-start | bytes 6291460
  6.5 14.8 %copy-start.2 = (s32[8]{0:T(128)S(1)}, s32[8]{0:T(128)}, u32[]{:S(2)}) copy-start(s32[8]{0:T(128)} %param.18) | copy-start | bytes 100
  6.5 16.6 %copy-start.3 = (bf16[128,8,128]{2,1,0:T(8,128)(2,1)S(1)}, bf16[128,8,128]{2,1,0:T(8,128)(2,1)}, u32[]{:S(2)}) copy-start(bf16[128,8,128]{2,1,0:T(8,128)(2,1)} %param.15) | copy-start | bytes 786436
  9.7 17.0 %all-to-all-start = ((bf16[4,128,256]{2,1,0:T(8,128)(2,1)}), bf16[4,128,256]{2,1,0:T(8,128)(2,1)S(1)}, u32[]{:S(2)}, u32[]{:S(2)}) async-start(bf16[4,128,256]{2,1,0:T(8,128)(2,1)} %copy.72), calls=%async_computation | async-start | bytes 524288 | tf_op jit(solution)/shard_map/all_to_all | solution.py:50
  16.1 49.4 %all-gather.4.cloned.1.call-start = ((), (), s32[]{:S(2)}) async-start(), calls=%async_computation.3 | async-start | bytes 1310720 | tf_op jit(solution)/shard_map/all_gather | solution.py:72
  31.3 0.7 collective-permute-start
  32.0 0.7 copy-start.5
  32.7 36.3 %copy-start.8 = (bf16[1024]{0:T(1024)(128)(2,1)S(1)}, bf16[1024]{0:T(1024)(128)(2,1)}, u32[]{:S(2)}) copy-start(bf16[1024]{0:T(1024)(128)(2,1)} %param.23) | copy-start | bytes 6148
  32.7 36.3 %copy-start.7 = (s32[128,8]{0,1:T(8,128)S(1)}, s32[128,8]{0,1:T(8,128)}, u32[]{:S(2)}) copy-start(s32[128,8]{0,1:T(8,128)} %param.27) | copy-start | bytes 12292
  32.7 63.7 %copy-start.4 = (bf16[128,1024]{1,0:T(8,128)(2,1)S(1)}, bf16[128,1024]{1,0:T(8,128)(2,1)}, u32[]{:S(2)}) copy-start(bf16[128,1024]{1,0:T(8,128)(2,1)} %param.21) | copy-start | bytes 786436
  32.8 64.8 %copy-start.6 = (bf16[1024,16]{0,1:T(8,128)(2,1)S(1)}, bf16[1024,16]{0,1:T(8,128)(2,1)}, u32[]{:S(2)}) copy-start(bf16[1024,16]{0,1:T(8,128)(2,1)} %param.24) | copy-start | bytes 98308
  32.8 63.6 %reduce-scatter.3.cloned.1.call-start = ((), (), s32[]{:S(2)}) async-start(), calls=%async_computation.4 | async-start | bytes 1310720 | tf_op jit(solution)/shard_map/reduce_scatter | solution.py:79
  69.0 115.4 %all-gather.6.cloned.1.call-start = ((), (), s32[]{:S(2)}) async-start(), calls=%async_computation.6 | async-start | bytes 1474560 | tf_op jit(solution)/shard_map/all_gather | solution.py:315
  105.5 157.5 %reduce-scatter.5.cloned.1.call-start = ((), (), s32[]{:S(2)}) async-start(), calls=%async_computation.5 | async-start | bytes 1310720 | tf_op jit(solution)/shard_map/reduce_scatter | solution.py:349
  235.2 29.5 %copy-start.1 = (bf16[1024,1024]{1,0:T(8,128)(2,1)S(1)}, bf16[1024,1024]{1,0:T(8,128)(2,1)}, u32[]{:S(2)}) copy-start(bf16[1024,1024]{1,0:T(8,128)(2,1)} %param.22) | copy-start | bytes 6291460
Sparse Core Ops, SparseCore 0:
  32.8 32.5 all-gather.3
  69.1 27.2 reduce-scatter.2
  105.6 28.5 all-gather.5
  236.9 26.0 reduce-scatter.4

commit v3 on v2

--- a/solution.py
+++ b/solution.py
@@ -62,10 +62,14 @@
     return (keys, values, valid)
 
 
-def project(attended, out_proj):
+def project(attended, out_proj, w_gate_up):
     lanes = lax.axis_size("tp")
     groups = lax.axis_size("ep")
     length = attended.shape[0]
+    halves = None
+    if lanes == 4:
+        attended, whole = lax.optimization_barrier((attended, w_gate_up))
+        halves = (whole[:, :, 0], whole[:, :, 1])
     if lanes == groups:
         swap = [(e * lanes + t, t * lanes + e) for e in range(groups) for t in range(lanes)]
         block = lax.ppermute(attended, ("ep", "tp"), swap)
@@ -75,15 +79,18 @@
         split = jnp.swapaxes(all_heads.reshape(length, groups, -1), 0, 1)
         tokens = lax.all_to_all(split, "ep", split_axis=0, concat_axis=0, tiled=True)
         tokens = tokens.reshape(groups * length, -1)
+    if halves is not None:
+        tokens, halves = lax.optimization_barrier((tokens, halves))
     part = jnp.dot(tokens, out_proj, preferred_element_type=jnp.float32)
-    return lax.psum_scatter(
+    summed = lax.psum_scatter(
         part.astype(jnp.bfloat16), "ep", scatter_dimension=0, tiled=True
     ).astype(jnp.float32)
+    return summed, halves
 
 
 def expert_kernel(
-    tokens, w_in_hbm, w_out_hbm, result,
-    w_in, w_out, sent, first, pair, second, acts,
+    tokens, w_gate_hbm, w_up_hbm, w_out_hbm, result,
+    w_gate, w_up, w_out, sent, first, pair, second, acts,
     load_in, load_out, send_sem, recv_sem,
 ):
     count, rows, _ = tokens.shape
@@ -93,7 +100,9 @@
     partner = chip * 2 + (1 - core)
     across = (1 - chip) * 2 + core
     loads_in = [
-        pltpu.make_async_copy(w_in_hbm.at[e], w_in.at[e], load_in.at[e]) for e in range(count)
+        pltpu.make_async_copy(source.at[e], target.at[e], load_in.at[kind, e])
+        for e in range(count)
+        for kind, (source, target) in enumerate(((w_gate_hbm, w_gate), (w_up_hbm, w_up)))
     ]
     loads_out = [
         pltpu.make_async_copy(w_out_hbm.at[e], w_out.at[e], load_out.at[e]) for e in range(count)
@@ -129,13 +138,19 @@
     ]
 
     def multiply_in(e):
-        loads_in[e].wait()
+        loads_in[2 * e].wait()
+        loads_in[2 * e + 1].wait()
+        width = w_gate.shape[2] // 4
 
         def block(i, carry):
-            part = jnp.dot(
-                tokens[e], w_in[e, i // 2, i % 2], preferred_element_type=jnp.float32
-            )
-            sent[e, i // 2, i % 2] = part.astype(jnp.bfloat16)
+            columns = pl.ds(pl.multiple_of(i * width, width), width)
+            for kind, weights in enumerate((w_gate, w_up)):
+                part = jnp.dot(
+                    tokens[e], weights[e, :, columns], preferred_element_type=jnp.float32
+                )
+                sent[e, i % 2, i // 2, :, kind * width : (kind + 1) * width] = part.astype(
+                    jnp.bfloat16
+                )
             return carry
 
         lax.fori_loop(0, 4, block, 0)
@@ -184,15 +199,12 @@
             copy.wait_send()
 
 
-def feed_forward(arrived, w_gate_up, w_down):
+def feed_forward(arrived, w_gate_up, halves, w_down):
     count, rows, width = arrived.shape
     lanes = lax.axis_size("tp")
     hidden_here = HID // lanes
     if lanes == 4:
-        w_in = w_gate_up.reshape(count, width, 2, 2, 2, hidden_here)
-        w_in = jnp.transpose(w_in, (0, 4, 3, 1, 2, 5)).reshape(
-            count, 2, 2, width, 2 * hidden_here
-        )
+        w_gate, w_up = halves
         bf16 = jnp.bfloat16
         return pl.pallas_call(
             expert_kernel,
@@ -201,17 +213,19 @@
                 pl.BlockSpec(memory_space=pltpu.VMEM),
                 pl.BlockSpec(memory_space=pl.ANY),
                 pl.BlockSpec(memory_space=pl.ANY),
+                pl.BlockSpec(memory_space=pl.ANY),
             ],
             out_specs=pl.BlockSpec(memory_space=pltpu.VMEM),
             scratch_shapes=[
-                pltpu.VMEM(w_in.shape, bf16),
+                pltpu.VMEM(w_gate.shape, bf16),
+                pltpu.VMEM(w_up.shape, bf16),
                 pltpu.VMEM(w_down.shape, bf16),
                 pltpu.VMEM((count, 2, 2, rows, 2 * hidden_here), bf16),
                 pltpu.VMEM((count, 2, rows, 2 * hidden_here), bf16),
                 pltpu.VMEM((count, rows, 2 * hidden_here), bf16),
                 pltpu.VMEM((count, rows, 2 * hidden_here), bf16),
                 pltpu.VMEM((count, 2, 2, rows, hidden_here), bf16),
-                pltpu.SemaphoreType.DMA((count,)),
+                pltpu.SemaphoreType.DMA((2, count)),
                 pltpu.SemaphoreType.DMA((count,)),
                 pltpu.SemaphoreType.DMA((5, count)),
                 pltpu.SemaphoreType.DMA((5, count)),
@@ -219,7 +233,7 @@
             compiler_params=pltpu.CompilerParams(
                 collective_id=1, has_side_effects=True, vmem_limit_bytes=50 << 20
             ),
-        )(arrived, w_in, w_down)
+        )(arrived, w_gate, w_up, w_down)
     term = jnp.einsum("erd,edgh->hegr", arrived, w_gate_up, preferred_element_type=jnp.float32)
     summed = lax.psum_scatter(
         term.astype(jnp.bfloat16), "tp", scatter_dimension=0, tiled=True
@@ -284,7 +298,7 @@
         .astype(jnp.bfloat16)
     )
     width_here = hidden.shape[1]
-    projected = project(attended, out_proj)
+    projected, halves = project(attended, out_proj, w_gate_up)
     residual_wide = narrow(hidden.astype(jnp.float32) + projected).astype(jnp.float32)
     gain = norm_gain.astype(jnp.float32)
     squares, logit_part = lax.psum(
@@ -338,7 +352,7 @@
     ).astype(jnp.bfloat16)
     rows = groups * capacity
     arrived = arrived.reshape(local_experts, rows, width_here)
-    expert_out = feed_forward(arrived, w_gate_up, w_down)
+    expert_out = feed_forward(arrived, w_gate_up, halves, w_down)
     weights = jnp.stack([picks * share_high[:, :, None, :], picks * share_low[:, :, None, :]])
     partial = jnp.einsum(
         "psecn,escd->snd",

time: 273 us -> 221 us (0.81)
  local copies, waits for them, and re-layouts: 90.3 us -> 27.3 us
  waiting for transfers between devices: 86.3 us -> 98.2 us
    reshape x3 -> x0, local copies, waits for them, and re-layouts: 78.7 us -> none  [the longest x2 51.7 us: feed_forward(): w_in = w_gate_up.reshape(count, width, 2, 2, 2, hidden_here)]
    all_gather x1, waiting for transfers between devices: 0.01 us -> 28.5 us  [per_device(): lax.all_gather(jnp.concatenate([normed, notes], axis=1), 'ep', axis=0)]
    all_gather x1, waiting for transfers between devices: 32.7 us -> 15.2 us  [project(): tokens = lax.all_gather(block, 'tp', axis=0, tiled=True)]
    optimization_barrier x0 -> x1, local copies, waits for them, and re-layouts: none -> 11 us  [project(): attended, whole = lax.optimization_barrier((attended, w_gate_up))]
    squeeze x0 -> x1, local copies, waits for them, and re-layouts: none -> 6.16 us  [project(): halves = (whole[:, :, 0], whole[:, :, 1])]
  transfers between devices with their start and end apart: 6 -> 6, of which waited for: 3 -> 5; matrix products, arithmetic and copies ran while one was open for 33% -> 12% of each run, Pallas kernels for 0% -> 0%
where the time goes in v3:
time: 221 us; the launch traced here: 220 us
  waiting for transfers between devices  98.2 us (44%)
  Pallas kernels  45.6 us (21%)
  local copies, waits for them, and re-layouts  27.3 us (12%)
  between operations  13.5 us (6%)
  other arithmetic  11.5 us (5%)
  matrix products  10.2 us (5%)
  starting transfers between devices  7.33 us (3%)
  blocking collectives  6.4 us (3%)
    pallas_call x1, Pallas kernels, feed_forward(): pl.pallas_call(expert_kernel, out_shape=jax.ShapeDtypeStruct(arrived.shap...  45.6 us
    all_gather x1, waiting for transfers between devices, per_device(): lax.all_gather(jnp.concatenate([normed, notes], axis=1), 'ep', axis=0)  28.5 us
    reduce_scatter x1, waiting for transfers between devices, project(): lax.psum_scatter(part.astype(jnp.bfloat16), 'ep', scatter_dimension=0, ti...  27.7 us
    reduce_scatter x1, waiting for transfers between devices, per_device(): lax.psum_scatter(partial.astype(jnp.bfloat16).reshape(groups * length, wi...  26.4 us
    all_gather x1, waiting for transfers between devices, project(): tokens = lax.all_gather(block, 'tp', axis=0, tiled=True)  15.2 us
    optimization_barrier x1, local copies, waits for them, and re-layouts, project(): attended, whole = lax.optimization_barrier((attended, w_gate_up))  11 us
    psum x1, blocking collectives, per_device(): lax.psum((jnp.sum(residual_wide * residual_wide, axis=1), jnp.dot(residua...  6.4 us
    all_to_all x1, starting transfers between devices, fetch_context(): lax.all_to_all(sending, 'ep', split_axis=0, concat_axis=0, tiled=True)  6.35 us
  transfers between devices with their start and end apart: 6, of which 5 were waited for; matrix products, arithmetic and copies ran while one was open for 12% of the time, Pallas kernels for 0%

profile of v3, /device:TPU:0, one launch (start us, length us, event | category | flops | bytes accessed | tf_op | source)
XLA Modules:
  0.0 220.1 jit_solution(15417484454965884126)
XLA Ops:
  6.5 1.1 constant_dynamic-slice_fusion.3
  7.8 0.8 convert_reduce_fusion.1
  9.0 0.7 copy.76
  9.7 6.3 %all-to-all-start = ((bf16[4,128,256]{2,1,0:T(8,128)(2,1)}), bf16[4,128,256]{2,1,0:T(8,128)(2,1)S(1)}, u32[]{:S(2)}, u32[]{:S(2)}) async-start(bf16[4,128,256]{2,1,0:T(8,128)(2,1)} %copy.76), calls=%async_computation | async-start | bytes 524288 | tf_op jit(solution)/shard_map/all_to_all | solution.py:50
  16.1 0.7 fusion.63
  16.8 0.7 constant_dynamic-slice_fusion.2
  17.5 0.7 fusion.75
  18.2 2.5 %compare_select_fusion.1 = s32[512,1]{0,1:T(1,128)S(1)} fusion(s32[512,1]{0,1:T(1,128)S(1)} %bitcast.128, s32[512,1]{0,1:T(1,128)S(1)} %bitcast.129, s32[]{:T(128)} %bitcast.11, s32[]{:T(128)} %bitcast.12, s32[]{:T(128)} %bitcast.14, s32[]{:T(128)} %bitcast.13), kind=kLoop, calls=%fused_computation.93 | loop fusion | flops 4096 | bytes 6160 | tf_op jit(solution)/shard_map/jit(_take)/gather | solution.py:54
  20.7 0.9 constant_dynamic-slice_fusion.1
  21.7 0.6 add_convert_fusion.3
  22.4 0.6 gather_fusion
  23.8 0.9 subtract_convert_fusion
  26.8 1.6 fusion.4
  28.9 0.8 fusion.16
  29.7 0.7 collective-permute-start
  30.5 0.7 copy-done.4
  31.2 11.0 %copy.86 = bf16[4,1024,2,1024]{3,1,0,2:T(8,128)(2,1)S(1)} copy(bf16[4,1024,2,1024]{3,2,1,0:T(2,128)(2,1)} %param.25) | data formatting | bytes 33554432 | tf_op jit(solution)/shard_map/optimization_barrier | solution.py:71
  42.3 6.2 %slice_bitcast_fusion = (bf16[4,1024,1024]{2,1,0:T(8,128)(2,1)}, bf16[4,1024,1024]{2,1,0:T(8,128)(2,1)}) fusion(bf16[4,1024,2,1024]{3,1,0,2:T(8,128)(2,1)S(1)} %copy.86), kind=kLoop, calls=%fused_computation.2 | loop fusion | bytes 33554432 | tf_op jit(solution)/shard_map/squeeze | solution.py:72
  48.4 15.2 %all-gather.4.cloned.1.call-done = bf16[512,1024]{0,1:T(8,128)(2,1)} async-done(((bf16[128,1024]{0,1:T(8,128)(2,1)}), bf16[512,1024]{0,1:T(8,128)(2,1)}) %all-gather.4.cloned.1.call-update) | async-done | bytes 1048592 | tf_op jit(solution)/shard_map/all_gather | solution.py:76
  63.7 3.6 %convolution_convert_fusion = bf16[512,1024]{1,0:T(8,128)(2,1)} fusion(bf16[512,1024]{0,1:T(8,128)(2,1)} %all-gather.4.cloned.1.call-done, bf16[1024,1024]{1,0:T(8,128)(2,1)S(1)} %copy-done), kind=kOutput, calls=%fused_computation.13 | convolution fusion | flops 1074266112 | bytes 4194304 | tf_op jit(solution)/shard_map/dot_general | solution.py:84
  67.3 27.7 %reduce-scatter.3.cloned.1.call-done = bf16[128,1024]{1,0:T(8,128)(2,1)} async-done(((bf16[512,1024]{1,0:T(8,128)(2,1)}), bf16[128,1024]{1,0:T(8,128)(2,1)}) %reduce-scatter.3.cloned.1.call-update) | async-done | bytes 262160 | tf_op jit(solution)/shard_map/reduce_scatter | solution.py:85
  95.1 1.0 add_convert_fusion
  96.6 6.4 %all-reduce.1 = (f32[128,16]{0,1:T(8,128)S(1)}, f32[128]{0:T(128)S(1)}) all-reduce(f32[128,16]{0,1:T(8,128)S(1)} %fusion.24, f32[128]{0:T(128)S(1)} %fusion.21), channel_id=1, replica_groups=mesh['grp'=2,'ep'=4,'tp'=4] {'tp'}, use_global_device_ids=true, to_apply=%region_7.8 | all-reduce | flops 2176 | bytes 17408 | tf_op jit(solution)/shard_map/psum | solution.py:304
  103.4 0.8 fusion.28
  104.4 28.5 %all-gather.6.cloned.1.call-done = bf16[512,1152]{1,0:T(8,128)(2,1)} async-done(((bf16[128,1152]{1,0:T(8,128)(2,1)}), bf16[512,1152]{1,0:T(8,128)(2,1)}) %all-gather.6.cloned.1.call-update) | async-done | bytes 1179664 | tf_op jit(solution)/shard_map/all_gather | solution.py:329
  132.9 1.2 dynamic-slice_bitcast_fusion.1
  134.4 1.9 convert_bitcast_fusion
  136.4 1.5 copy.92
  138.3 45.6 %shard_map.127 = bf16[4,256,1024]{2,1,0:T(8,128)(2,1)S(1)} custom-call(bf16[4,256,1024]{2,1,0:T(8,128)(2,1)} %bitcast.122, bf16[4,1024,1024]{2,1,0:T(8,128)(2,1)} %get-tuple-element.25.w_gate_hbm, bf16[4,1024,1024]{2,1,0:T(8,128)(2,1)} %get-tuple-element.26.w_up_hbm, bf16[4,1024,1024]{2,1,0:T(8,128)(2,1)} %w_out_hbm.1), custom_call_target="tpu_custom_call" | custom-call | tf_op jit(solution)/shard_map/pallas_call | solution.py:209
  184.0 1.5 bitcast_convert_fusion
  185.5 26.4 %reduce-scatter.5.cloned.1.call-done = bf16[128,1024]{1,0:T(8,128)(2,1)} async-done(((bf16[512,1024]{1,0:T(8,128)(2,1)}), bf16[128,1024]{1,0:T(8,128)(2,1)}) %reduce-scatter.5.cloned.1.call-update) | async-done | bytes 262160 | tf_op jit(solution)/shard_map/reduce_scatter | solution.py:363
  211.9 1.7 fusion.25
  (75 shorter events, 5.9 us)
Async XLA Ops:
  6.5 57.1 %copy-start = (bf16[1024,1024]{1,0:T(8,128)(2,1)S(1)}, bf16[1024,1024]{1,0:T(8,128)(2,1)}, u32[]{:S(2)}) copy-start(bf16[1024,1024]{1,0:T(8,128)(2,1)} %param.22) | copy-start | bytes 6291460
  6.5 15.8 %copy-start.2 = (bf16[128,8,128]{2,1,0:T(8,128)(2,1)S(1)}, bf16[128,8,128]{2,1,0:T(8,128)(2,1)}, u32[]{:S(2)}) copy-start(bf16[128,8,128]{2,1,0:T(8,128)(2,1)} %param.15) | copy-start | bytes 786436
  6.5 15.9 %copy-start.1 = (s32[8]{0:T(128)S(1)}, s32[8]{0:T(128)}, u32[]{:S(2)}) copy-start(s32[8]{0:T(128)} %param.18) | copy-start | bytes 100
  9.7 15.3 %all-to-all-start = ((bf16[4,128,256]{2,1,0:T(8,128)(2,1)}), bf16[4,128,256]{2,1,0:T(8,128)(2,1)S(1)}, u32[]{:S(2)}, u32[]{:S(2)}) async-start(bf16[4,128,256]{2,1,0:T(8,128)(2,1)} %copy.76), calls=%async_computation | async-start | bytes 524288 | tf_op jit(solution)/shard_map/all_to_all | solution.py:50
  16.1 47.6 %all-gather.4.cloned.1.call-start = ((), (), s32[]{:S(2)}) async-start(), calls=%async_computation.3 | async-start | bytes 1310720 | tf_op jit(solution)/shard_map/all_gather | solution.py:76
  29.7 0.7 collective-permute-start
  30.4 0.7 copy-start.4
  31.2 63.9 %reduce-scatter.3.cloned.1.call-start = ((), (), s32[]{:S(2)}) async-start(), calls=%async_computation.4 | async-start | bytes 1310720 | tf_op jit(solution)/shard_map/reduce_scatter | solution.py:85
  63.6 3.6 %copy-start.7 = (bf16[1024]{0:T(1024)(128)(2,1)S(1)}, bf16[1024]{0:T(1024)(128)(2,1)}, u32[]{:S(2)}) copy-start(bf16[1024]{0:T(1024)(128)(2,1)} %param.23) | copy-start | bytes 6148
  63.6 3.7 %copy-start.6 = (s32[128,8]{0,1:T(8,128)S(1)}, s32[128,8]{0,1:T(8,128)}, u32[]{:S(2)}) copy-start(s32[128,8]{0,1:T(8,128)} %param.27) | copy-start | bytes 12292
  63.6 31.5 %copy-start.3 = (bf16[128,1024]{1,0:T(8,128)(2,1)S(1)}, bf16[128,1024]{1,0:T(8,128)(2,1)}, u32[]{:S(2)}) copy-start(bf16[128,1024]{1,0:T(8,128)(2,1)} %param.21) | copy-start | bytes 786436
  63.6 32.6 %copy-start.5 = (bf16[1024,16]{0,1:T(8,128)(2,1)S(1)}, bf16[1024,16]{0,1:T(8,128)(2,1)}, u32[]{:S(2)}) copy-start(bf16[1024,16]{0,1:T(8,128)(2,1)} %param.24) | copy-start | bytes 98308
  67.2 65.7 %all-gather.6.cloned.1.call-start = ((), (), s32[]{:S(2)}) async-start(), calls=%async_computation.6 | async-start | bytes 1474560 | tf_op jit(solution)/shard_map/all_gather | solution.py:329
  104.2 107.7 %reduce-scatter.5.cloned.1.call-start = ((), (), s32[]{:S(2)}) async-start(), calls=%async_computation.5 | async-start | bytes 1310720 | tf_op jit(solution)/shard_map/reduce_scatter | solution.py:363
Sparse Core Ops, SparseCore 0:
  31.3 32.2 all-gather.3
  67.3 27.6 reduce-scatter.2
  104.3 28.6 all-gather.5
  185.6 26.2 reduce-scatter.4
